TPU v7x, 128 devices: a whole 4x4x4 slice. The times are simulated.
128 devices in a mesh: seq: 16 (over z_lo, x, core), db: 8 (over y, z_hi).
Axes of the slice: x: 4, y: 4, z: 4 (z_hi: 2, z_lo: 2; z = z_hi * 2 + z_lo), core: 2. Of those that a mesh axis runs over, the one named last changes fastest.
Arguments:
- hidden_in: bfloat16 [4096, 4096], P('seq'), may hold values from -4 to 4
- query_rows: bfloat16 [4096, 4096], P('seq', 'db'), may hold values from -32 to 32
- key_rows: bfloat16 [4096, 4096], P('seq', 'db'), may hold values from -32 to 32
- value_rows: bfloat16 [4096, 4096], P('seq', 'db'), may hold values from -6 to 6
- w_self_out: bfloat16 [4096, 4096], P('db'), may hold values from -0.1796875 to 0.1796875
- norm_gain: bfloat16 [4096], replicated, may hold values from 0.099609375 to 1.8984375
- w_cross_q: bfloat16 [4096, 4096], P(None, 'db'), may hold values from -2 to 2
- w_cross_k: bfloat16 [1024, 4096], P(None, 'db'), may hold values from -1 to 1
- w_cross_v: bfloat16 [1024, 4096], P(None, 'db'), may hold values from -0.1875 to 0.1875
- w_cross_out: bfloat16 [4096, 4096], P('db'), may hold values from -0.09375 to 0.09375
- enc_table: bfloat16 [64, 128, 1024], P('db'), may hold values from -6 to 6
- nb_shard: int32 [64, 2], P('seq'), may hold values from 0 to 7, all different within a row; in each aligned block of 4 rows (0 to 3, 4 to 7, ...) at most 2 rows name the same one
- nb_row: int32 [64, 2], P('seq'), may hold values from 0 to 7
Outputs:
- block_out: float32 [4096, 4096], P(('seq', 'db'))
Inputs may be any that keep to these rules, and one draw needn't show every extreme that they name: `nb_shard`: the spans held by one index of seq name each shard at most 2 times, and in the spans of some indices one shard exactly 2 times; the 2 neighbours of a span lie in different shards.
All inputs are finite; a program needn't handle non-finite values.
Results may differ from a plain program's by a relative error of at most 0.038.
Values may be sent and summed in bfloat16 or wider, within the bound.
A program may use at most 128 MiB of HBM per device.

v0:
```python
import math
import jax
import jax.numpy as jnp
from jax import lax
from jax.sharding import PartitionSpec as P

HD = 128
SPAN = 64
NEIGH = 2
NLEN = 128
NEG_BIG = -1e30


def from_behind(block, axis, distance):
    devices = range(lax.axis_size(axis))
    route = [(i - distance, i) for i in devices if i - distance in devices]
    return lax.ppermute(block, axis, route)


def attend_block(state, query_three, key_block, value_block, query_pos, key_pos, score_scale):
    run_max, run_sum, run_acc = state
    scores = (
        jnp.einsum("qhd,khd->hqk", query_three, key_block, preferred_element_type=jnp.float32)
        * score_scale
    )
    allowed = (key_pos[None, :] <= query_pos[:, None]) & (key_pos[None, :] >= 0)
    scores = jnp.where(allowed[None], scores, NEG_BIG)
    new_max = jnp.maximum(run_max, jnp.max(scores, axis=-1))
    rescale = jnp.exp(run_max - new_max)
    weights = jnp.exp(scores - new_max[..., None])
    new_sum = run_sum * rescale + jnp.sum(weights, axis=-1)
    added = jnp.einsum(
        "hqk,khd->hqd",
        weights.astype(jnp.bfloat16),
        value_block,
        preferred_element_type=jnp.float32,
    )
    return (new_max, new_sum, run_acc * rescale[..., None] + added)


def fold_piece(carried, query_three, pieces, query_pos, score_scale):
    key_piece, value_piece = pieces
    count_rows = key_piece.shape[0]
    heads_local = query_three.shape[1]
    block_rows = math.gcd(count_rows, 512)
    block_count = count_rows // block_rows
    last_query = query_pos[query_pos.shape[0] - 1]

    def one_block(block_index, state):
        key_first = block_index * block_rows

        def compute(inner):
            key_block = lax.dynamic_slice_in_dim(
                key_piece, block_index * block_rows, block_rows, 0
            ).reshape(block_rows, heads_local, HD)
            value_block = lax.dynamic_slice_in_dim(
                value_piece, block_index * block_rows, block_rows, 0
            ).reshape(block_rows, heads_local, HD)
            key_pos = key_first + jnp.arange(block_rows, dtype=jnp.int32)
            return attend_block(
                inner, query_three, key_block, value_block, query_pos, key_pos, score_scale
            )

        def unchanged(inner):
            return inner

        live = (key_first <= last_query) & (key_first + block_rows > 0)
        return lax.cond(live, compute, unchanged, state)

    return lax.fori_loop(0, block_count, one_block, carried)


def empty_state(heads_local, rows):
    return (
        jnp.full((heads_local, rows), NEG_BIG, jnp.float32),
        jnp.zeros((heads_local, rows), jnp.float32),
        jnp.zeros((heads_local, rows, HD), jnp.float32),
    )


def finish_state(state, rows, width_local):
    run_max, run_sum, run_acc = state
    return (
        (run_acc / run_sum[..., None])
        .transpose(1, 0, 2)
        .reshape(rows, width_local)
        .astype(jnp.bfloat16)
    )


def per_device(
    hidden_in,
    query_rows,
    key_rows,
    value_rows,
    w_self_out,
    norm_gain,
    w_cross_q,
    w_cross_k,
    w_cross_v,
    w_cross_out,
    enc_table,
    nb_shard,
    nb_row,
):
    tok_rows = hidden_in.shape[0]
    width_local = query_rows.shape[1]
    heads_local = width_local // HD
    db_count = lax.axis_size("db")
    seq_index = lax.axis_index("seq")
    db_index = lax.axis_index("db")
    score_scale = 1.0 / math.sqrt(HD)
    query_three = query_rows.reshape(tok_rows, heads_local, HD)
    query_pos = seq_index * tok_rows + jnp.arange(tok_rows, dtype=jnp.int32)
    initial = empty_state(heads_local, tok_rows)
    state = fold_piece(
        initial,
        query_three,
        (
            lax.all_gather(key_rows, "seq", axis=0, tiled=True),
            lax.all_gather(value_rows, "seq", axis=0, tiled=True),
        ),
        query_pos,
        score_scale,
    )
    attended = finish_state(state, tok_rows, width_local)
    share_rows = tok_rows // db_count
    attn_total = lax.psum(
        jnp.dot(attended, w_self_out, preferred_element_type=jnp.float32).astype(jnp.bfloat16), "db"
    ).astype(jnp.float32)
    residual = hidden_in.astype(jnp.float32) + attn_total
    mean_square = jnp.mean(residual * residual, axis=-1, keepdims=True)
    normed = (residual * lax.rsqrt(mean_square + 1e-05) * norm_gain.astype(jnp.float32)).astype(
        jnp.bfloat16
    )
    cross_query = jnp.dot(normed, w_cross_q, preferred_element_type=jnp.float32).astype(
        jnp.bfloat16
    )
    span_count = tok_rows // SPAN
    entry_count = span_count * NEIGH
    capacity = 2 * ((entry_count + db_count - 1) // db_count)
    shard_flat = nb_shard.reshape(entry_count)
    row_flat = nb_row.reshape(entry_count)
    entry_ids = jnp.arange(entry_count, dtype=jnp.int32)
    earlier = (shard_flat[:, None] == shard_flat[None, :]) & (
        entry_ids[None, :] < entry_ids[:, None]
    )
    rank_flat = jnp.sum(earlier.astype(jnp.int32), axis=1)
    slot_ids = jnp.arange(capacity, dtype=jnp.int32)
    chosen = ((shard_flat[None, :] == db_index) & (rank_flat[None, :] == slot_ids[:, None])).astype(
        jnp.int32
    )
    pick_rows = jnp.sum(chosen * row_flat[None, :], axis=1)
    live_slot = jnp.sum(chosen, axis=1) > 0
    picked = jnp.take(enc_table, pick_rows, axis=0)
    outgoing = jnp.where(live_slot[:, None, None], picked, jnp.zeros_like(picked))
    arrived = lax.all_gather(outgoing, "db", axis=0, tiled=True)
    wanted = jnp.take(arrived, shard_flat * capacity + rank_flat, axis=0).reshape(
        entry_count * NLEN, enc_table.shape[2]
    )
    cross_keys = jnp.dot(wanted, w_cross_k, preferred_element_type=jnp.float32).astype(jnp.bfloat16)
    cross_values = jnp.dot(wanted, w_cross_v, preferred_element_type=jnp.float32).astype(
        jnp.bfloat16
    )
    cross_pair = jnp.stack((cross_keys, cross_values)).reshape(
        2, span_count, NEIGH * NLEN, width_local
    )
    previous = from_behind(cross_pair[:, span_count - 1], "seq", 1)
    extended = jnp.concatenate((previous[:, None], cross_pair), axis=1).reshape(
        2, span_count + 1, NEIGH * NLEN, heads_local, HD
    )
    padded = jnp.pad(cross_query, ((1, SPAN - 1), (0, 0))).reshape(
        span_count + 1, SPAN, heads_local, HD
    )
    scores = (
        jnp.einsum("gqhd,gkhd->ghqk", padded, extended[0], preferred_element_type=jnp.float32)
        * score_scale
    )
    top_score = jnp.max(scores, axis=-1, keepdims=True)
    weights = jnp.exp(scores - top_score)
    totals = jnp.sum(weights, axis=-1, keepdims=True)
    mixed = (
        jnp.einsum(
            "ghqk,gkhd->ghqd",
            weights.astype(jnp.bfloat16),
            extended[1],
            preferred_element_type=jnp.float32,
        )
        / totals
    )
    cross_mixed = (
        mixed.transpose(0, 2, 1, 3)
        .reshape((span_count + 1) * SPAN, width_local)[1 : tok_rows + 1]
        .astype(jnp.bfloat16)
    )
    cross_share = lax.psum_scatter(
        jnp.dot(cross_mixed, w_cross_out, preferred_element_type=jnp.float32).astype(jnp.bfloat16),
        "db",
        scatter_dimension=0,
        tiled=True,
    ).astype(jnp.float32)
    own_residual = lax.dynamic_slice_in_dim(residual, db_index * share_rows, share_rows, 0)
    return own_residual + cross_share


def solution(mesh):
    placed = (
        P("seq", None),
        P("seq", "db"),
        P("seq", "db"),
        P("seq", "db"),
        P("db", None),
        P(),
        P(None, "db"),
        P(None, "db"),
        P(None, "db"),
        P("db", None),
        P("db", None, None),
        P("seq", None),
        P("seq", None),
    )
    return jax.shard_map(
        per_device, mesh=mesh, in_specs=placed, out_specs=P(("seq", "db"), None), check_vma=False
    )
```

profile of v0, /device:TPU:0, one launch (start us, length us, event | category | flops | bytes accessed | tf_op | source)
XLA Modules:
  0.0 419.2 jit_solution(12266112979966981673)
XLA Ops:
  6.6 0.9 copy.65
  7.5 0.1 mul.94
  7.6 0.8 copy.64
  8.3 0.1 reshape.166
  8.4 0.2 convert_reduce_fusion
  8.6 0.1 convert_reduce_fusion.1
  8.8 0.6 gather_fusion
  9.4 0.9 select_select_fusion
  10.3 0.0 all-gather.8.cloned.1.call-update
  10.4 0.0 all-gather.4.cloned.1.call-start
  10.4 0.8 copy.59
  11.3 0.0 all-gather.4.cloned.1.call-update
  11.3 0.0 all-gather.6.cloned.1.call-start
  11.3 0.8 copy.61
  12.2 0.0 all-gather.6.cloned.1.call-update
  12.2 0.0 all-reduce.3.cloned.1.call-start
  12.3 0.1 copy.66
  12.4 0.1 mul.98
  12.5 0.7 slice.18
  13.1 0.1 copy.60
  13.3 0.2 copy.62
  13.5 0.1 broadcast_bitcast_fusion
  13.5 71.1 %all-gather.8.cloned.1.call-done = bf16[16,128,1024]{2,1,0:T(8,128)(2,1)} async-done(((bf16[2,128,1024]{2,1,0:T(8,128)(2,1)}), bf16[16,128,1024]{2,1,0:T(8,128)(2,1)}) %all-gather.8.cloned.1.call-update) | async-done | bytes 4194320 | tf_op jit(solution)/shard_map/all_gather | solution.py:157
  84.6 2.9 gather_fusion.1
  87.5 41.5 %all-gather.4.cloned.1.call-done = bf16[4096,512]{0,1:T(8,128)(2,1)} async-done(((bf16[256,512]{0,1:T(8,128)(2,1)}), bf16[4096,512]{0,1:T(8,128)(2,1)}) %all-gather.4.cloned.1.call-update) | async-done | bytes 4194320 | tf_op jit(solution)/shard_map/all_gather | solution.py:120
  129.0 46.8 %all-gather.6.cloned.1.call-done = bf16[4096,512]{0,1:T(8,128)(2,1)} async-done(((bf16[256,512]{0,1:T(8,128)(2,1)}), bf16[4096,512]{0,1:T(8,128)(2,1)}) %all-gather.6.cloned.1.call-update) | async-done | bytes 4194320 | tf_op jit(solution)/shard_map/all_gather | solution.py:121
  175.8 8.5 %while.18 = (s32[]{:T(128)}, f32[4,256]{1,0:T(4,128)S(1)}, f32[4,256]{1,0:T(4,128)S(1)}, f32[4,256,128]{2,1,0:T(8,128)S(1)}, s32[]{:T(128)}, /*index=5*/bf16[409...) while((s32[]{:T(128)}, f32[4,256]{1,0:T(4,128)S(1)}, ...), condition=%wide.region_5.6_spmd.clone, body=%wide.region_0.5_spmd.clone.sunk | while | flops 272633600 | bytes 11085173 | solution.py:70
  176.4 3.1 conditional.3
  176.5 0.2 compare_and_fusion
  176.7 1.3 constant_dynamic-slice_fusion
  178.0 0.6 fusion.22
  178.6 0.3 fusion.3
  178.9 0.6 convolution_add_fusion
  184.3 0.2 copy.63
  184.6 4.8 %convolution_convert_fusion.1 = bf16[256,4096]{1,0:T(8,128)(2,1)} fusion(bf16[256,512]{0,1:T(8,128)(2,1)S(1)} %bitcast.62, bf16[512,4096]{1,0:T(8,128)(2,1)} %param.21), kind=kOutput, calls=%fused_computation.18 | convolution fusion | flops 1074790400 | bytes 6553600 | tf_op jit(solution)/shard_map/dot_general | solution.py:129
  189.4 0.0 all-reduce.3.cloned.1.call-update
  189.4 0.0 reduce-scatter.2.cloned.1.call-start
  189.5 0.4 bitcast_select_fusion.1
  189.9 0.8 copy-done.12
  190.7 1.2 convolution_convert_fusion.3
  191.9 0.1 copy-done.4
  192.0 0.5 copy.67
  192.5 3.1 convolution_convert_fusion.2
  195.6 0.5 copy.68
  196.1 0.1 fusion.16
  196.2 2.4 collective-permute-start
  198.6 1.3 collective-permute-done
  199.9 0.3 maximum_maximum_fusion
  200.2 0.2 fusion.23
  200.4 121.6 %all-reduce.3.cloned.1.call-done = bf16[256,4096]{1,0:T(8,128)(2,1)} async-done(((bf16[256,4096]{1,0:T(8,128)(2,1)}), bf16[256,4096]{1,0:T(8,128)(2,1)}) %all-reduce.3.cloned.1.call-update) | async-done | bytes 2097168 | tf_op jit(solution)/shard_map/psum | solution.py:128
  322.0 5.2 %convert_add_fusion = (f32[256,4096]{1,0:T(8,128)}, f32[256]{0:T(256)S(1)}) fusion(bf16[256,4096]{1,0:T(8,128)(2,1)} %all-reduce.3.cloned.1.call-done, bf16[256,4096]{1,0:T(8,128)(2,1)} %param.17), kind=kLoop, calls=%fused_computation.21 | loop fusion | flops 5242624 | bytes 8389632 | tf_op jit(solution)/shard_map/add | solution.py:131
  327.2 1.0 copy-done.10
  328.2 1.3 fusion.11
  329.5 0.1 pad.4
  329.6 0.1 reshape.165
  329.7 0.4 fusion.24
  330.1 0.5 fusion.12
  330.6 0.7 fusion.10
  331.2 0.3 copy.73
  331.6 1.2 copy-done.11
  332.8 2.6 convolution_convert_fusion
  335.4 0.0 reduce-scatter.2.cloned.1.call-update
  335.4 75.3 %reduce-scatter.2.cloned.1.call-done = bf16[32,4096]{1,0:T(8,128)(2,1)} async-done(((bf16[256,4096]{1,0:T(8,128)(2,1)}), bf16[32,4096]{1,0:T(8,128)(2,1)}) %reduce-scatter.2.cloned.1.call-update) | async-done | bytes 262160 | tf_op jit(solution)/shard_map/reduce_scatter | solution.py:196
  410.7 2.0 convert_add_fusion.1
  (59 shorter events, 0.4 us)
Async XLA Ops:
  6.5 2.3 copy-start
  6.5 3.9 copy-start.5
  6.5 4.8 %copy-start.6 = (bf16[256,512]{1,0:T(8,128)(2,1)S(1)}, bf16[256,512]{1,0:T(8,128)(2,1)}, u32[]{:S(2)}) copy-start(bf16[256,512]{1,0:T(8,128)(2,1)} %param.20) | copy-start | bytes 786436
  6.5 78.1 %all-gather.8.cloned.1.call-start = ((), (), s32[]{:S(2)}) async-start(), calls=%async_computation.4 | async-start | bytes 4718592 | tf_op jit(solution)/shard_map/all_gather | solution.py:157
  8.8 3.5 copy-start.9
  8.8 4.3 %copy-start.7 = (bf16[256,512]{1,0:T(8,128)(2,1)S(1)}, bf16[256,512]{1,0:T(8,128)(2,1)}, u32[]{:S(2)}) copy-start(bf16[256,512]{1,0:T(8,128)(2,1)} %param.18) | copy-start | bytes 786436
  10.4 118.6 %all-gather.4.cloned.1.call-start = ((), (), s32[]{:S(2)}) async-start(), calls=%async_computation.1 | async-start | bytes 4456448 | tf_op jit(solution)/shard_map/all_gather | solution.py:120
  11.3 164.5 %all-gather.6.cloned.1.call-start = ((), (), s32[]{:S(2)}) async-start(), calls=%async_computation.2 | async-start | bytes 4456448 | tf_op jit(solution)/shard_map/all_gather | solution.py:121
  12.2 309.8 %all-reduce.3.cloned.1.call-start = ((), (), s32[]{:S(2)}) async-start(), calls=%async_computation.3 | async-start | bytes 4194304 | tf_op jit(solution)/shard_map/psum | solution.py:128
  189.4 1.2 copy-start.12
  189.4 221.3 %reduce-scatter.2.cloned.1.call-start = ((), (), s32[]{:S(2)}) async-start(), calls=%async_computation.5 | async-start | bytes 2359296 | tf_op jit(solution)/shard_map/reduce_scatter | solution.py:196
  190.7 1.3 copy-start.4
  195.6 3.0 copy-start.8
  196.2 3.7 collective-permute-start
  322.0 5.2 %copy-start.2 = (bf16[256,4096]{1,0:T(8,128)(2,1)S(1)}, bf16[256,4096]{1,0:T(8,128)(2,1)}, u32[]{:S(2)}) copy-start(bf16[256,4096]{1,0:T(8,128)(2,1)} %param.17) | copy-start | bytes 6291460
  322.0 5.2 %copy-start.3 = (bf16[256,4096]{1,0:T(8,128)(2,1)S(1)}, bf16[256,4096]{1,0:T(8,128)(2,1)}, u32[]{:S(2)}) copy-start(bf16[256,4096]{1,0:T(8,128)(2,1)} %all-reduce.3.cloned.1.call-done) | copy-start | bytes 6291460
  322.0 6.2 %copy-start.10 = (bf16[4096,512]{1,0:T(8,128)(2,1)S(1)}, bf16[4096,512]{1,0:T(8,128)(2,1)}, u32[]{:S(2)}) copy-start(bf16[4096,512]{1,0:T(8,128)(2,1)} %param.23) | copy-start | bytes 12582916
  330.6 2.2 copy-start.11
  332.8 79.9 %copy-start.1 = (bf16[8,128,1024]{2,1,0:T(8,128)(2,1)S(1)}, bf16[8,128,1024]{2,1,0:T(8,128)(2,1)}, u32[]{:S(2)}) copy-start(bf16[8,128,1024]{2,1,0:T(8,128)(2,1)} %param.27) | copy-start | bytes 6291460
Sparse Core Ops, SparseCore 0:
  10.5 74.0 all-gather.7
  86.2 42.6 all-gather.3
  130.6 45.1 all-gather.5
  189.5 132.3 all-reduce.2
  335.5 75.1 reduce-scatter.1
where the time goes:
time: 420 us; the launch traced here: 419 us
  waiting for transfers between devices  358 us (85%)
  matrix products  15.3 us (4%)
  local copies, waits for them, and re-layouts  14.5 us (3%)
  between operations  13.5 us (3%)
  other arithmetic  10.3 us (2%)
  loops' own time  5.49 us (1%)
    psum x1, waiting for transfers between devices, per_device(): lax.psum(jnp.dot(attended, w_self_out, preferred_element_type=jnp.float32...  122 us
    reduce_scatter x1, waiting for transfers between devices, per_device(): lax.psum_scatter(jnp.dot(cross_mixed, w_cross_out, preferred_element_type...  75.3 us
    all_gather x1, waiting for transfers between devices, per_device(): arrived = lax.all_gather(outgoing, 'db', axis=0, tiled=True)  71.1 us
    all_gather x1, waiting for transfers between devices, per_device(): lax.all_gather(value_rows, 'seq', axis=0, tiled=True)  46.8 us
    all_gather x1, waiting for transfers between devices, per_device(): lax.all_gather(key_rows, 'seq', axis=0, tiled=True)  41.5 us
  transfers between devices with their start and end apart: 6, of which 6 were waited for; matrix products, arithmetic and copies ran while one was open for 3% of the time, Pallas kernels for 0%

commit v1 on v0

--- a/solution.py
+++ b/solution.py
@@ -125,8 +125,12 @@
     )
     attended = finish_state(state, tok_rows, width_local)
     share_rows = tok_rows // db_count
-    attn_total = lax.psum(
-        jnp.dot(attended, w_self_out, preferred_element_type=jnp.float32).astype(jnp.bfloat16), "db"
+    attn_total = jnp.sum(
+        lax.all_gather(
+            jnp.dot(attended, w_self_out, preferred_element_type=jnp.float32).astype(jnp.bfloat16),
+            "db",
+        ),
+        axis=0,
     ).astype(jnp.float32)
     residual = hidden_in.astype(jnp.float32) + attn_total
     mean_square = jnp.mean(residual * residual, axis=-1, keepdims=True)

time: 420 us -> 470 us (1.12)
  waiting for transfers between devices: 358 us -> 396 us
  other arithmetic: 10.3 us -> 18.6 us
    all_gather x0 -> x1, waiting for transfers between devices: none -> 174 us  [per_device(): lax.all_gather(jnp.dot(attended, w_self_out, preferred_element_type=jnp.f...]
    psum x1 -> x0, waiting for transfers between devices: 122 us -> none  [per_device(): lax.psum(jnp.dot(attended, w_self_out, preferred_element_type=jnp.float32...]
    all_gather x1, waiting for transfers between devices: 71.1 us -> 59.1 us  [per_device(): arrived = lax.all_gather(outgoing, 'db', axis=0, tiled=True)]
    reduce_sum x0 -> x1, other arithmetic: none -> 9.16 us  [per_device(): jnp.sum(lax.all_gather(jnp.dot(attended, w_self_out, preferred_element_ty...]
  transfers between devices with their start and end apart: 6 -> 6, of which waited for: 6 -> 6; matrix products, arithmetic and copies ran while one was open for 3% -> 5% of each run, Pallas kernels for 0% -> 0%
where the time goes in v1:
time: 470 us; the launch traced here: 469 us
  waiting for transfers between devices  396 us (84%)
  other arithmetic  18.6 us (4%)
  local copies, waits for them, and re-layouts  17.6 us (4%)
  matrix products  15.4 us (3%)
  between operations  13.4 us (3%)
  loops' own time  5.89 us (1%)
    all_gather x1, waiting for transfers between devices, per_device(): lax.all_gather(jnp.dot(attended, w_self_out, preferred_element_type=jnp.f...  174 us
    reduce_scatter x1, waiting for transfers between devices, per_device(): lax.psum_scatter(jnp.dot(cross_mixed, w_cross_out, preferred_element_type...  73.4 us
    all_gather x1, waiting for transfers between devices, per_device(): arrived = lax.all_gather(outgoing, 'db', axis=0, tiled=True)  59.1 us
    all_gather x1, waiting for transfers between devices, per_device(): lax.all_gather(value_rows, 'seq', axis=0, tiled=True)  46.8 us
    all_gather x1, waiting for transfers between devices, per_device(): lax.all_gather(key_rows, 'seq', axis=0, tiled=True)  41.3 us
  transfers between devices with their start and end apart: 6, of which 6 were waited for; matrix products, arithmetic and copies ran while one was open for 5% of the time, Pallas kernels for 0%

profile of v1, /device:TPU:0, one launch (start us, length us, event | category | flops | bytes accessed | tf_op | source)
XLA Modules:
  0.0 469.1 jit_solution(8208925755443001170)
XLA Ops:
  6.5 2.0 copy.59
  8.5 0.0 all-gather.6.cloned.1.call-update
  8.6 0.0 all-gather.8.cloned.1.call-start
  8.6 1.8 copy.61
  10.4 0.0 all-gather.8.cloned.1.call-update
  10.4 0.0 all-gather.10.cloned.1.call-start
  10.5 0.8 copy.64
  11.3 0.1 reshape.166
  11.3 0.8 copy.65
  12.1 0.1 mul.94
  12.2 0.2 convert_reduce_fusion
  12.4 0.2 convert_reduce_fusion.1
  12.6 0.6 gather_fusion
  13.2 0.9 select_select_fusion
  14.1 0.0 all-gather.12.cloned.1.call-start
  14.2 0.6 slice.18
  14.8 0.1 copy.60
  15.0 0.2 copy.62
  15.1 41.3 %all-gather.6.cloned.1.call-done = bf16[4096,512]{0,1:T(8,128)(2,1)} async-done(((bf16[256,512]{0,1:T(8,128)(2,1)}), bf16[4096,512]{0,1:T(8,128)(2,1)}) %all-gather.6.cloned.1.call-update) | async-done | bytes 4194320 | tf_op jit(solution)/shard_map/all_gather | solution.py:120
  56.5 46.8 %all-gather.8.cloned.1.call-done = bf16[4096,512]{0,1:T(8,128)(2,1)} async-done(((bf16[256,512]{0,1:T(8,128)(2,1)}), bf16[4096,512]{0,1:T(8,128)(2,1)}) %all-gather.8.cloned.1.call-update) | async-done | bytes 4194320 | tf_op jit(solution)/shard_map/all_gather | solution.py:121
  103.3 9.0 %while.18 = (s32[]{:T(128)}, f32[4,256]{1,0:T(4,128)S(1)}, f32[4,256]{1,0:T(4,128)S(1)}, f32[4,256,128]{2,1,0:T(8,128)S(1)}, s32[]{:T(128)}, /*index=5*/bf16[409...) while((s32[]{:T(128)}, f32[4,256]{1,0:T(4,128)S(1)}, ...), condition=%wide.region_5.6_spmd.clone, body=%wide.region_0.5_spmd.clone.sunk | while | flops 272633600 | bytes 11085165 | solution.py:70
  104.0 3.1 conditional.3
  104.0 1.3 constant_dynamic-slice_fusion
  105.4 0.2 compare_and_fusion
  105.6 0.6 fusion.22
  106.1 0.3 fusion.3
  106.5 0.7 convolution_add_fusion
  112.3 0.2 copy.63
  112.5 4.8 %convolution_convert_fusion.1 = bf16[256,4096]{1,0:T(8,128)(2,1)} fusion(bf16[256,512]{0,1:T(8,128)(2,1)S(1)} %bitcast.64, bf16[512,4096]{1,0:T(8,128)(2,1)} %param.21), kind=kOutput, calls=%fused_computation.18 | convolution fusion | flops 1074790400 | bytes 6553600 | tf_op jit(solution)/shard_map/dot_general | solution.py:130
  117.3 0.0 all-gather.12.cloned.1.call-update
  117.4 0.0 reduce-scatter.2.cloned.1.call-start
  117.4 0.6 copy-done.7
  118.0 0.1 copy.66
  118.1 0.1 mul.98
  118.2 0.1 broadcast_bitcast_fusion
  118.3 59.1 %all-gather.10.cloned.1.call-done = bf16[16,128,1024]{2,1,0:T(8,128)(2,1)} async-done(((bf16[2,128,1024]{2,1,0:T(8,128)(2,1)}), bf16[16,128,1024]{2,1,0:T(8,128)(2,1)}) %all-gather.10.cloned.1.call-update) | async-done | bytes 4194320 | tf_op jit(solution)/shard_map/all_gather | solution.py:161
  177.4 2.9 gather_fusion.1
  180.3 0.4 bitcast_select_fusion.1
  180.7 0.8 copy-done.10
  181.5 1.2 convolution_convert_fusion.3
  182.7 0.1 copy-done.3
  182.8 0.5 copy.67
  183.3 3.1 convolution_convert_fusion.2
  186.5 0.5 copy.68
  187.0 0.1 fusion.16
  187.1 1.6 collective-permute-start
  188.6 1.3 collective-permute-done
  189.9 0.3 maximum_maximum_fusion
  190.2 1.3 fusion.23
  191.5 174.4 %all-gather.12.cloned.1.call-done = bf16[2048,4096]{1,0:T(8,128)(2,1)} async-done(((bf16[256,4096]{1,0:T(8,128)(2,1)}), bf16[2048,4096]{1,0:T(8,128)(2,1)}) %all-gather.12.cloned.1.call-update) | async-done | bytes 16777232 | tf_op jit(solution)/shard_map/all_gather | solution.py:129
  365.9 9.2 %reduce_sum.70 = bf16[256,4096]{1,0:T(8,128)(2,1)S(1)} reduce(bf16[8,256,4096]{2,1,0:T(8,128)(2,1)} %bitcast.60, bf16[]{:T(256)} %constant.91.clone.1), dimensions={0}, to_apply=%region_6.7 | reduce | flops 7340032 | bytes 18874370 | tf_op jit(solution)/shard_map/reduce_sum | solution.py:128
  375.1 4.4 convert_add_fusion
  379.5 1.4 fusion.11
  380.9 0.1 pad.4
  381.0 0.1 reshape.165
  381.1 0.4 fusion.24
  381.5 0.5 fusion.12
  382.0 0.4 copy-done.4
  382.4 0.7 fusion.10
  383.0 0.3 copy.73
  383.4 1.2 copy-done.9
  384.6 2.6 convolution_convert_fusion
  387.2 73.4 %reduce-scatter.2.cloned.1.call-done = bf16[32,4096]{1,0:T(8,128)(2,1)} async-done(((bf16[256,4096]{1,0:T(8,128)(2,1)}), bf16[32,4096]{1,0:T(8,128)(2,1)}) %reduce-scatter.2.cloned.1.call-update) | async-done | bytes 262160 | tf_op jit(solution)/shard_map/reduce_scatter | solution.py:200
  460.6 2.0 convert_add_fusion.1
  (56 shorter events, 0.4 us)
Async XLA Ops:
  6.5 6.0 %copy-start = (bf16[8,128,1024]{2,1,0:T(8,128)(2,1)S(1)}, bf16[8,128,1024]{2,1,0:T(8,128)(2,1)}, u32[]{:S(2)}) copy-start(bf16[8,128,1024]{2,1,0:T(8,128)(2,1)} %param.27) | copy-start | bytes 6291460
  6.5 8.3 %copy-start.5 = (bf16[256,512]{1,0:T(8,128)(2,1)S(1)}, bf16[256,512]{1,0:T(8,128)(2,1)}, u32[]{:S(2)}) copy-start(bf16[256,512]{1,0:T(8,128)(2,1)} %param.18) | copy-start | bytes 786436
  6.5 49.9 %all-gather.6.cloned.1.call-start = ((), (), s32[]{:S(2)}) async-start(), calls=%async_computation.1 | async-start | bytes 4456448 | tf_op jit(solution)/shard_map/all_gather | solution.py:120
  8.6 94.7 %all-gather.8.cloned.1.call-start = ((), (), s32[]{:S(2)}) async-start(), calls=%async_computation.2 | async-start | bytes 4456448 | tf_op jit(solution)/shard_map/all_gather | solution.py:121
  10.4 167.0 %all-gather.10.cloned.1.call-start = ((), (), s32[]{:S(2)}) async-start(), calls=%async_computation.3 | async-start | bytes 4718592 | tf_op jit(solution)/shard_map/all_gather | solution.py:161
  14.1 351.8 %all-gather.12.cloned.1.call-start = ((), (), s32[]{:S(2)}) async-start(), calls=%async_computation.5 | async-start | bytes 18874368 | tf_op jit(solution)/shard_map/all_gather | solution.py:129
  117.3 0.7 copy-start.7
  117.4 343.3 %reduce-scatter.2.cloned.1.call-start = ((), (), s32[]{:S(2)}) async-start(), calls=%async_computation.4 | async-start | bytes 2359296 | tf_op jit(solution)/shard_map/reduce_scatter | solution.py:200
  180.3 1.2 copy-start.10
  181.5 1.3 copy-start.3
  186.5 2.2 copy-start.6
  187.1 2.9 collective-permute-start
  375.1 4.4 copy-start.2
  375.1 4.4 copy-start.8
  381.1 1.3 copy-start.4
  382.4 2.2 copy-start.9
  384.6 78.0 %copy-start.1 = (bf16[8,128,1024]{2,1,0:T(8,128)(2,1)S(1)}, bf16[8,128,1024]{2,1,0:T(8,128)(2,1)}, u32[]{:S(2)}) copy-start(bf16[8,128,1024]{2,1,0:T(8,128)(2,1)} %param.27) | copy-start | bytes 6291460
Sparse Core Ops, SparseCore 0:
  9.0 47.4 all-gather.5
  58.1 45.1 all-gather.7
  105.6 71.7 all-gather.9
  179.6 186.3 all-gather.11
  387.3 73.2 reduce-scatter.1
